TPU v7x, 128 devices: a whole 4x4x4 slice. The times are simulated.
128 devices in a mesh: expert: 64 (over y, z, x), half: 2 (over core).
Axes of the slice: x: 4, y: 4, z: 4, core: 2. Of those that a mesh axis runs over, the one named last changes fastest.
Arguments:
- hidden_in: bfloat16 [8192, 2048], P('expert'), may hold values from -6 to 6
- modality: int32 [8192], replicated, may hold values from 0 to 1, as said below
- expert_ids: int32 [8192, 8], P('expert'), may hold values from 0 to 63, all different within a row; in each aligned block of 128 rows (0 to 127, 128 to 255, ...) at most 24 rows name the same one
- route_weights: float32 [8192, 8], P('expert'), may hold values from 0.03 to 0.3
- w_gate_up: bfloat16 [128, 2048, 2, 768], P('expert', None, None, 'half'), may hold values from -0.125 to 0.125
- w_down: bfloat16 [128, 768, 2048], P('expert', 'half'), may hold values from -0.21875 to 0.21875
- norm_gain: float32 [2048], replicated, may hold values from 0.1 to 1.9
- w_query: bfloat16 [2048, 4096], P(None, 'half'), may hold values from -1 to 1
- key_value_weight: bfloat16 [2048, 2, 512], P(None, None, 'half'), may hold values from -1 to 1
- q_gain: float32 [128], replicated, may hold values from 1 to 8
- k_gain: float32 [128], replicated, may hold values from 1 to 8
Outputs:
- hidden_out: float32 [8192, 2048], P('expert')
- attended: bfloat16 [8192, 4096], P('expert', 'half')
Inputs may be any that keep to these rules, and one draw needn't show every extreme that they name: `modality`: constant over each aligned block of 128 tokens; both values occur. `expert_ids`: the 8 ids of a token differ; among the tokens of one aligned block of 128 no id is named more than 24 times, a bound that some block reaches.
All inputs are finite; a program needn't handle non-finite values.
Results may differ from a plain program's by a relative error of at most 0.03.
The roundings to bfloat16 on the way count: a program that leaves them out, or rounds other values in their place, can miss the bound.
Values may be sent and summed in bfloat16 or wider, within the bound.
A program may use at most 128 MiB of HBM per device.

v0:
```python
import math
import jax
import jax.numpy as jnp
from jax import lax
from jax.sharding import PartitionSpec as P

EPSILON = 1e-06


def from_partner(block, axis, stride):
    count = lax.axis_size(axis)
    route = []
    for low in range(count):
        high = low | 1 << stride
        if high != low and high < count:
            route += [(low, high), (high, low)]
    return lax.ppermute(block, axis, route)


def rms_scale(values, gain_row):
    mean_sq = jnp.mean(values * values, axis=-1, keepdims=True)
    return values * lax.rsqrt(mean_sq + EPSILON) * gain_row


def expert_pass(received, source_kind, w_gate_up, w_down):
    groups, slots, model_width = received.shape
    ordering = jnp.argsort(source_kind, stable=True)
    restore = jnp.argsort(ordering, stable=True)
    text_count = jnp.sum((source_kind == 0).astype(jnp.int32))
    group_sizes = jnp.stack([text_count * slots, (groups - text_count) * slots])
    rows_sorted = received[ordering].reshape(groups * slots, model_width)
    local_experts = w_gate_up.shape[0]
    half_units = w_gate_up.shape[3]
    gate_up = lax.ragged_dot(
        rows_sorted,
        w_gate_up.reshape(local_experts, model_width, 2 * half_units),
        group_sizes,
        preferred_element_type=jnp.float32,
    )
    activated = (jax.nn.silu(gate_up[:, :half_units]) * gate_up[:, half_units:]).astype(
        jnp.bfloat16
    )
    partial_out = lax.ragged_dot(activated, w_down, group_sizes, preferred_element_type=jnp.float32)
    return partial_out.reshape(groups, slots, model_width)[restore]


def body(
    hidden_in,
    modality,
    expert_ids,
    route_weights,
    w_gate_up,
    w_down,
    norm_gain,
    w_query,
    key_value_weight,
    q_gain,
    k_gain,
):
    tok_rows, model_width = hidden_in.shape
    top_count = expert_ids.shape[1]
    groups = lax.axis_size("expert")
    capacity = max(2, 3 * tok_rows * top_count // (2 * groups))
    source_kind = modality.reshape(groups, tok_rows)[:, 0]
    flat_ids = expert_ids.reshape(-1)
    row_total = tok_rows * top_count
    one_hot = (flat_ids[:, None] == jnp.arange(groups, dtype=jnp.int32)[None, :]).astype(jnp.int32)
    slot_rank = jnp.sum((jnp.cumsum(one_hot, axis=0) - one_hot) * one_hot, axis=1)
    slot_index = flat_ids * capacity + slot_rank
    row_token = jnp.arange(row_total, dtype=jnp.int32) // top_count
    slot_token = jnp.full((groups * capacity,), tok_rows, jnp.int32).at[slot_index].set(row_token)
    padded_in = jnp.concatenate([hidden_in, jnp.zeros((1, model_width), hidden_in.dtype)], axis=0)
    outgoing = padded_in[slot_token].reshape(groups, capacity, model_width)
    partial_out = expert_pass(
        lax.all_to_all(outgoing, "expert", split_axis=0, concat_axis=0, tiled=True),
        source_kind,
        w_gate_up,
        w_down,
    )
    combined = partial_out + from_partner(partial_out, "half", 0)
    returned = lax.all_to_all(
        combined.astype(jnp.bfloat16), "expert", split_axis=0, concat_axis=0, tiled=True
    )
    part_width = returned.shape[2]
    gathered = (
        returned.reshape(groups * capacity, part_width)[slot_index]
        .astype(jnp.float32)
        .reshape(tok_rows, top_count, part_width)
    )
    mixture = jnp.sum(gathered * route_weights[:, :, None], axis=1)
    hidden_out = hidden_in.astype(jnp.float32) + mixture
    normalized_input = rms_scale(hidden_out, norm_gain).astype(jnp.bfloat16)
    head_dim = q_gain.shape[0]
    queries = jnp.dot(normalized_input, w_query, preferred_element_type=jnp.float32)
    local_heads = queries.shape[1] // head_dim
    queries = rms_scale(queries.reshape(tok_rows, local_heads, head_dim), q_gain).astype(
        jnp.bfloat16
    )
    kv_width = key_value_weight.shape[2]
    kv_heads = kv_width // head_dim
    key_value_rows = jnp.dot(
        normalized_input,
        key_value_weight.reshape(model_width, 2 * kv_width),
        preferred_element_type=jnp.float32,
    ).reshape(tok_rows, 2, kv_heads, head_dim)
    keys_local = rms_scale(key_value_rows[:, 0], k_gain).astype(jnp.bfloat16)
    values_local = key_value_rows[:, 1].astype(jnp.bfloat16)
    stacked = jnp.stack([keys_local, values_local], axis=1).reshape(tok_rows, 2, kv_width)
    queries_per_group = local_heads // kv_heads
    query_rows = queries_per_group * tok_rows
    grouped_queries = (
        queries.reshape(tok_rows, kv_heads, queries_per_group, head_dim)
        .transpose(1, 2, 0, 3)
        .reshape(kv_heads, query_rows, head_dim)
    )
    score_scale = head_dim ** (-0.5)
    initial = (
        jnp.full((kv_heads, query_rows), -1e30, jnp.float32),
        jnp.zeros((kv_heads, query_rows), jnp.float32),
        jnp.zeros((kv_heads, query_rows, head_dim), jnp.float32),
    )
    kv_piece = lax.all_gather(stacked, "expert", axis=0, tiled=True)
    key_rows = kv_piece.shape[0]
    key_block = math.gcd(key_rows, 1024)
    blocks = kv_piece.reshape(key_rows // key_block, key_block, 2, kv_heads, head_dim)

    def step_block(inner_state, kv_block):
        peak_in, totals_in, accum_in = inner_state
        scores = (
            jnp.einsum(
                "hrd,khd->hrk", grouped_queries, kv_block[:, 0], preferred_element_type=jnp.float32
            )
            * score_scale
        )
        new_peak = jnp.maximum(peak_in, jnp.max(scores, axis=-1))
        weights = jnp.exp(scores - new_peak[..., None])
        rescale = jnp.exp(peak_in - new_peak)
        totals_out = totals_in * rescale + jnp.sum(weights, axis=-1)
        accum_out = accum_in * rescale[..., None] + jnp.einsum(
            "hrk,khd->hrd",
            weights.astype(jnp.bfloat16),
            kv_block[:, 1],
            preferred_element_type=jnp.float32,
        )
        return ((new_peak, totals_out, accum_out), None)

    final_state = lax.scan(step_block, initial, blocks)[0]
    accumulated = final_state[2] / final_state[1][..., None]
    attended = (
        accumulated.reshape(kv_heads, queries_per_group, tok_rows, head_dim)
        .transpose(2, 0, 1, 3)
        .reshape(tok_rows, local_heads * head_dim)
        .astype(jnp.bfloat16)
    )
    return (hidden_out, attended)


def solution(mesh):
    in_specs = (
        P("expert", None),
        P(),
        P("expert", None),
        P("expert", None),
        P("expert", None, None, "half"),
        P("expert", "half", None),
        P(),
        P(None, "half"),
        P(None, None, "half"),
        P(),
        P(),
    )
    out_specs = (P("expert", None), P("expert", "half"))
    return jax.shard_map(body, mesh=mesh, in_specs=in_specs, out_specs=out_specs, check_vma=False)
```

profile of v0, /device:TPU:0, one launch (start us, length us, event | category | flops | bytes accessed | tf_op | source)
XLA Modules:
  0.0 562.9 jit_solution(2645386171560433740)
XLA Ops:
  8.9 18.0 %reduce-window.6 = s32[64,8,128]{2,1,0:T(8,128)S(1)} reduce-window(s32[64,8,128]{2,1,0:T(8,128)S(1)} %fusion.22, s32[]{:T(128)} %constant.32.clone.1), window={size=1x1x128 pad=0_0x0_0x127_0}, to_apply=%region_0.0 | reduce-window | flops 8323072 | bytes 524292 | tf_op jit(solution)/shard_map/reduce-window
  27.7 4.3 scatter_custom_fusion
  32.1 1.1 concatenate.4
  33.2 7.1 %gather_fusion = bf16[1536,2048]{1,0:T(8,128)(2,1)} fusion(bf16[129,2048]{1,0:T(8,128)(2,1)S(1)} %concatenate.4, s32[2048]{0:T(1024)S(1)} %pad_clamp_fusion), kind=kCustom, calls=%fused_computation | custom fusion | bytes 12589056 | tf_op jit(solution)/shard_map/gather | solution.py:73
  40.3 11.9 %all-to-all-start = ((bf16[64,24,2048]{2,1,0:T(8,128)(2,1)}), bf16[64,24,2048]{2,1,0:T(8,128)(2,1)}, u32[]{:S(2)}, u32[]{:S(2)}) async-start(bf16[64,24,2048]{2,1,0:T(8,128)(2,1)} %bitcast.107), calls=%async_computation | async-start | bytes 12582912 | tf_op jit(solution)/shard_map/all_to_all | solution.py:75
  52.3 2.0 sort.31
  56.8 1.3 ragged-dot-metadata
  58.2 14.6 %reshape.140 = bf16[2,2048,768]{2,1,0:T(8,128)(2,1)} reshape(bf16[2,2048,2,384]{3,2,1,0:T(2,128)(2,1)} %param.17) | data formatting | bytes 12582912 | tf_op jit(solution)/shard_map/reshape | solution.py:36
  72.8 2.0 sort.32
  74.8 57.0 %all-to-all-done = bf16[64,24,2048]{2,1,0:T(8,128)(2,1)} async-done(((bf16[64,24,2048]{2,1,0:T(8,128)(2,1)}), bf16[64,24,2048]{2,1,0:T(8,128)(2,1)}, u32[]{:S(2)}, u32[]{:S(2)}) %all-to-all-start) | async-done | bytes 6291488 | tf_op jit(solution)/shard_map/all_to_all | solution.py:75
  131.9 6.4 %gather_fusion.1 = bf16[64,24,2048]{2,1,0:T(8,128)(2,1)} fusion(bf16[64,24,2048]{2,1,0:T(8,128)(2,1)} %all-to-all-done, s32[1024]{0:T(1024)S(1)} %pad_clamp_fusion.2), kind=kCustom, calls=%fused_computation.1 | custom fusion | bytes 12583168 | tf_op jit(solution)/shard_map/gather | solution.py:31
  138.2 13.9 %ragged-dot-none.1 = f32[1536,768]{1,0:T(8,128)} custom-call(s32[1]{0:T(128)} %get-tuple-element.41, s32[3]{0:T(128)} %get-tuple-element.42, s32[7]{0:T(128)} %get-tuple-element.43, s32[7]{0:T(128)} %get-tuple-element.44, s32[1]{0:T(128)} %get-tuple-element.41, bf16[1536,2048]{1,0:T(8,128)(2,1)} %bitcast.113, bf16[2,2048,768]{2,1,0:T(8,128)(2,1)} %reshape.140), custom_call_target="tpu_custom_call" | custom-call | flops 4831838208 | bytes 17301512 | tf_op jit(solution)/shard_map/ragged_dot_general/ragged-dot-none
  152.1 4.1 fusion.15
  156.2 12.3 %ragged-dot-none = f32[1536,2048]{1,0:T(8,128)} custom-call(s32[1]{0:T(128)} %get-tuple-element.41, s32[3]{0:T(128)} %get-tuple-element.42, s32[7]{0:T(128)} %get-tuple-element.43, s32[7]{0:T(128)} %get-tuple-element.44, s32[1]{0:T(128)} %get-tuple-element.41, bf16[1536,384]{1,0:T(8,128)(2,1)} %fusion.15, bf16[2,384,2048]{2,1,0:T(8,128)(2,1)} %param.18), custom_call_target="tpu_custom_call" | custom-call | flops 2415919104 | bytes 16908296 | tf_op jit(solution)/shard_map/ragged_dot_general/ragged-dot-none
  168.5 10.4 %gather_fusion.2 = f32[64,24,2048]{2,1,0:T(8,128)} fusion(f32[64,24,2048]{2,1,0:T(8,128)} %bitcast.105, s32[1024]{0:T(1024)S(1)} %pad_clamp_fusion.1), kind=kCustom, calls=%fused_computation.2 | custom fusion | bytes 25166080 | tf_op jit(solution)/shard_map/gather | solution.py:44
  178.9 19.4 %collective-permute-done = f32[64,24,2048]{2,1,0:T(8,128)S(1)} collective-permute-done((f32[64,24,2048]{2,1,0:T(8,128)}, f32[64,24,2048]{2,1,0:T(8,128)S(1)}, u32[]{:S(2)}, u32[]{:S(2)}) %collective-permute-start) | collective-permute-done | bytes 12582944 | tf_op jit(solution)/shard_map/ppermute | solution.py:17
  198.3 8.5 %add_convert_fusion = bf16[64,24,2048]{2,1,0:T(8,128)(2,1)} fusion(f32[64,24,2048]{2,1,0:T(8,128)} %gather_fusion.2, f32[64,24,2048]{2,1,0:T(8,128)S(1)} %collective-permute-done), kind=kLoop, calls=%fused_computation.25 | loop fusion | flops 6291456 | bytes 31457280 | tf_op jit(solution)/shard_map/convert_element_type | solution.py:82
  206.8 7.7 %all-to-all-start.1 = ((bf16[64,24,2048]{2,1,0:T(8,128)(2,1)}), bf16[64,24,2048]{2,1,0:T(8,128)(2,1)}, u32[]{:S(2)}, u32[]{:S(2)}) async-start(bf16[64,24,2048]{2,1,0:T(8,128)(2,1)} %add_convert_fusion), calls=%async_computation.1 | async-start | bytes 12582912 | tf_op jit(solution)/shard_map/all_to_all | solution.py:81
  214.5 10.4 %all-gather.2.cloned.1.call-start = ((), (), s32[]{:S(2)}) async-start(), calls=%async_computation.2 | async-start | bytes 8519680 | tf_op jit(solution)/shard_map/all_gather | solution.py:122
  225.0 2.0 copy.71
  227.1 2.5 copy.62
  229.5 66.1 %all-to-all-done.1 = bf16[64,24,2048]{2,1,0:T(8,128)(2,1)} async-done(((bf16[64,24,2048]{2,1,0:T(8,128)(2,1)}), bf16[64,24,2048]{2,1,0:T(8,128)(2,1)}, u32[]{:S(2)}, u32[]{:S(2)}) %all-to-all-start.1) | async-done | bytes 6291488 | tf_op jit(solution)/shard_map/all_to_all | solution.py:81
  295.7 12.5 %gather_fusion.3 = bf16[1024,2048]{1,0:T(8,128)(2,1)} fusion(bf16[1536,2048]{1,0:T(8,128)(2,1)} %bitcast.10, s32[1024]{0:T(1024)S(1)} %broadcast_clamp_fusion), kind=kCustom, calls=%fused_computation.3 | custom fusion | bytes 8392704 | tf_op jit(solution)/shard_map/gather | solution.py:86
  308.2 6.7 %fusion.14 = f32[128,2048]{1,0:T(8,128)S(1)} fusion(bf16[1024,2048]{1,0:T(8,128)(2,1)} %gather_fusion.3, f32[128,8]{1,0:T(8,128)S(1)} %copy.61), kind=kLoop, calls=%fused_computation.27 | loop fusion | flops 6029312 | bytes 5246976 | tf_op jit(solution)/shard_map/reduce_sum | solution.py:90
  316.8 4.7 fusion.29
  323.1 90.7 %all-gather.2.cloned.1.call-done = bf16[8192,2,256]{0,2,1:T(8,128)(2,1)} async-done(((bf16[128,2,256]{0,2,1:T(8,128)(2,1)}), bf16[8192,2,256]{0,2,1:T(8,128)(2,1)}) %all-gather.2.cloned.1.call-update) | async-done | bytes 8388624 | tf_op jit(solution)/shard_map/all_gather | solution.py:122
  413.8 16.5 %copy.72 = bf16[64,8,8,1024]{3,2,1,0:T(8,128)(2,1)} copy(bf16[64,8,8,1024]{3,1,2,0:T(8,128)(2,1)} %bitcast.110) | data formatting | bytes 16777216
  430.3 12.0 %copy.66 = bf16[8,1024,2,2,128]{4,1,3,2,0:T(8,128)(2,1)} copy(bf16[8,1024,2,2,128]{1,0,4,3,2:T(8,128)(2,1)} %bitcast.106) | data formatting | bytes 16777216
  442.3 111.7 %while.15 = (s32[]{:T(128)}, f32[2,1024]{1,0:T(2,128)S(1)}, f32[2,1024]{1,0:T(2,128)S(1)}, f32[2,1024,128]{2,1,0:T(8,128)S(1)}, bf16[8,1024,2,2,128]{4,1,3,2,0:T...) while((s32[]{:T(128)}, f32[2,1024]{1,0:T(2,128)S(1)}, ...), condition=%wide.region_14.15_spmd.clone, body=%wide.region_11.14_spmd.clone.sunk | while | flops 1091315712 | bytes 64618624 | solution.py:147
  442.3 1.3 dynamic-slice_bitcast_fusion.2
  443.6 4.5 bitcast_reduce_fusion.2
  448.1 4.9 fusion.42
  453.0 0.8 copy-done
  453.8 2.4 fusion.44
  456.2 1.3 dynamic-slice_bitcast_fusion.2
  457.6 4.5 bitcast_reduce_fusion.2
  462.0 4.9 fusion.42
  467.8 2.4 fusion.44
  470.2 1.3 dynamic-slice_bitcast_fusion.2
  471.5 4.5 bitcast_reduce_fusion.2
  476.0 4.9 fusion.42
  481.0 0.8 copy-done
  481.8 2.4 fusion.44
  484.2 1.3 dynamic-slice_bitcast_fusion.2
  485.5 4.5 bitcast_reduce_fusion.2
  490.0 4.9 fusion.42
  495.7 2.4 fusion.44
  498.2 1.3 dynamic-slice_bitcast_fusion.2
  499.5 4.5 bitcast_reduce_fusion.2
  503.9 4.9 fusion.42
  509.7 2.4 fusion.44
  512.1 1.3 dynamic-slice_bitcast_fusion.2
  513.4 4.5 bitcast_reduce_fusion.2
  517.9 4.9 fusion.42
  523.7 2.4 fusion.44
  526.1 1.3 dynamic-slice_bitcast_fusion.2
  527.4 4.5 bitcast_reduce_fusion.2
  531.9 4.9 fusion.42
  537.6 2.4 fusion.44
  540.1 1.3 dynamic-slice_bitcast_fusion.2
  541.4 4.5 bitcast_reduce_fusion.2
  545.8 4.9 fusion.42
  551.6 2.4 fusion.44
  554.7 0.9 copy.78
  (107 shorter events, 13.3 us)
Async XLA Ops:
  40.3 11.9 %copy-start.5 = (s32[8192]{0:T(1024)S(1)}, s32[8192]{0:T(1024)}, u32[]{:S(2)}) copy-start(s32[8192]{0:T(1024)} %param.14) | copy-start | bytes 98308
  40.3 91.6 %all-to-all-start = ((bf16[64,24,2048]{2,1,0:T(8,128)(2,1)}), bf16[64,24,2048]{2,1,0:T(8,128)(2,1)}, u32[]{:S(2)}, u32[]{:S(2)}) async-start(bf16[64,24,2048]{2,1,0:T(8,128)(2,1)} %bitcast.107), calls=%async_computation | async-start | bytes 12582912 | tf_op jit(solution)/shard_map/all_to_all | solution.py:75
  178.9 19.4 %collective-permute-start = (f32[64,24,2048]{2,1,0:T(8,128)}, f32[64,24,2048]{2,1,0:T(8,128)S(1)}, u32[]{:S(2)}, u32[]{:S(2)}) collective-permute-start(f32[64,24,2048]{2,1,0:T(8,128)} %gather_fusion.2), channel_id=1, source_target_pairs={{0,1},{1,0},{2,3},{3,2},{4,5},{5,4},{6,7},{7,6},{8,9},{9,8},{10,11... | collective-permute-start | bytes 37748744 | tf_op jit(solution)/shard_map/ppermute | solution.py:17
  206.8 18.1 %copy-start.6 = (f32[128,8]{0,1:T(8,128)S(1)}, f32[128,8]{0,1:T(8,128)}, u32[]{:S(2)}) copy-start(f32[128,8]{0,1:T(8,128)} %param.16) | copy-start | bytes 12292
  206.8 88.9 %all-to-all-start.1 = ((bf16[64,24,2048]{2,1,0:T(8,128)(2,1)}), bf16[64,24,2048]{2,1,0:T(8,128)(2,1)}, u32[]{:S(2)}, u32[]{:S(2)}) async-start(bf16[64,24,2048]{2,1,0:T(8,128)(2,1)} %add_convert_fusion), calls=%async_computation.1 | async-start | bytes 12582912 | tf_op jit(solution)/shard_map/all_to_all | solution.py:81
  214.5 199.3 %all-gather.2.cloned.1.call-start = ((), (), s32[]{:S(2)}) async-start(), calls=%async_computation.2 | async-start | bytes 8519680 | tf_op jit(solution)/shard_map/all_gather | solution.py:122
  295.7 19.1 %copy-start.3 = (bf16[128,2048]{1,0:T(8,128)(2,1)S(1)}, bf16[128,2048]{1,0:T(8,128)(2,1)}, u32[]{:S(2)}) copy-start(bf16[128,2048]{1,0:T(8,128)(2,1)} %param.13) | copy-start | bytes 1572868
  308.2 6.9 %copy-start.2 = (bf16[512,2048]{1,0:T(8,128)(2,1)S(1)}, bf16[512,2048]{1,0:T(8,128)(2,1)}, u32[]{:S(2)}) copy-start(bf16[512,2048]{1,0:T(8,128)(2,1)} %copy.62) | copy-start | bytes 6291460
  308.2 7.0 %copy-start.4 = (f32[2048]{0:T(1024)S(1)}, f32[2048]{0:T(1024)}, u32[]{:S(2)}) copy-start(f32[2048]{0:T(1024)} %param.19) | copy-start | bytes 24580
  308.2 7.8 %copy-start.8 = (f32[128]{0:T(128)S(1)}, f32[128]{0:T(128)}, u32[]{:S(2)}) copy-start(f32[128]{0:T(128)} %param.23) | copy-start | bytes 1540
  315.1 6.4 %copy-start.1 = (f32[128,2048]{1,0:T(8,128)}, f32[128,2048]{1,0:T(8,128)S(1)}, u32[]{:S(2)}) copy-start(f32[128,2048]{1,0:T(8,128)S(1)} %get-tuple-element.109) | copy-start | bytes 3145732
  321.5 1.1 copy-start.7
  448.1 5.8 %copy-start = (f32[2,1024,1024]{2,1,0:T(8,128)S(1)}, f32[2,1024,1024]{2,1,0:T(8,128)}, u32[]{:S(2)}) copy-start(f32[2,1024,1024]{2,1,0:T(8,128)} %get-tuple-element.154) | copy-start | bytes 25165828 | tf_op jit(solution)/shard_map/while
  462.0 5.8 %copy-start = (f32[2,1024,1024]{2,1,0:T(8,128)S(1)}, f32[2,1024,1024]{2,1,0:T(8,128)}, u32[]{:S(2)}) copy-start(f32[2,1024,1024]{2,1,0:T(8,128)} %get-tuple-element.154) | copy-start | bytes 25165828 | tf_op jit(solution)/shard_map/while
  476.0 5.8 %copy-start = (f32[2,1024,1024]{2,1,0:T(8,128)S(1)}, f32[2,1024,1024]{2,1,0:T(8,128)}, u32[]{:S(2)}) copy-start(f32[2,1024,1024]{2,1,0:T(8,128)} %get-tuple-element.154) | copy-start | bytes 25165828 | tf_op jit(solution)/shard_map/while
  490.0 5.8 %copy-start = (f32[2,1024,1024]{2,1,0:T(8,128)S(1)}, f32[2,1024,1024]{2,1,0:T(8,128)}, u32[]{:S(2)}) copy-start(f32[2,1024,1024]{2,1,0:T(8,128)} %get-tuple-element.154) | copy-start | bytes 25165828 | tf_op jit(solution)/shard_map/while
  503.9 5.8 %copy-start = (f32[2,1024,1024]{2,1,0:T(8,128)S(1)}, f32[2,1024,1024]{2,1,0:T(8,128)}, u32[]{:S(2)}) copy-start(f32[2,1024,1024]{2,1,0:T(8,128)} %get-tuple-element.154) | copy-start | bytes 25165828 | tf_op jit(solution)/shard_map/while
  517.9 5.8 %copy-start = (f32[2,1024,1024]{2,1,0:T(8,128)S(1)}, f32[2,1024,1024]{2,1,0:T(8,128)}, u32[]{:S(2)}) copy-start(f32[2,1024,1024]{2,1,0:T(8,128)} %get-tuple-element.154) | copy-start | bytes 25165828 | tf_op jit(solution)/shard_map/while
  531.9 5.8 %copy-start = (f32[2,1024,1024]{2,1,0:T(8,128)S(1)}, f32[2,1024,1024]{2,1,0:T(8,128)}, u32[]{:S(2)}) copy-start(f32[2,1024,1024]{2,1,0:T(8,128)} %get-tuple-element.154) | copy-start | bytes 25165828 | tf_op jit(solution)/shard_map/while
  545.8 5.8 %copy-start = (f32[2,1024,1024]{2,1,0:T(8,128)S(1)}, f32[2,1024,1024]{2,1,0:T(8,128)}, u32[]{:S(2)}) copy-start(f32[2,1024,1024]{2,1,0:T(8,128)} %get-tuple-element.154) | copy-start | bytes 25165828 | tf_op jit(solution)/shard_map/while
Sparse Core Ops, SparseCore 0:
  316.9 96.8 all-gather.1
where the time goes:
time: 573 us; the launch traced here: 563 us
  waiting for transfers between devices  233 us (41%)
  local copies, waits for them, and re-layouts  110 us (19%)
  other arithmetic  85.3 us (15%)
  matrix products  60.3 us (11%)
  starting transfers between devices  30 us (5%)
  Pallas kernels  27.5 us (5%)
  between operations  16.1 us (3%)
    all_gather x1, waiting for transfers between devices, body(): kv_piece = lax.all_gather(stacked, 'expert', axis=0, tiled=True)  90.7 us
    all_to_all x1, waiting for transfers between devices, body(): lax.all_to_all(combined.astype(jnp.bfloat16), 'expert', split_axis=0, con...  66.1 us
    all_to_all x1, waiting for transfers between devices, body(): lax.all_to_all(outgoing, 'expert', split_axis=0, concat_axis=0, tiled=True)  57 us
    reduce_sum x8, other arithmetic, step_block(): totals_out = totals_in * rescale + jnp.sum(weights, axis=-1)  39.3 us
    dot_general x8, matrix products, step_block(): jnp.einsum('hrd,khd->hrk', grouped_queries, kv_block[:, 0], preferred_ele...  35.7 us
    unnamed x24, local copies, waits for them, and re-layouts  32.8 us
    another operation x2, Pallas kernels  26.2 us
    ppermute x1, waiting for transfers between devices, from_partner(): return lax.ppermute(block, axis, route)  19.4 us
  transfers between devices with their start and end apart: 4, of which 4 were waited for; matrix products, arithmetic and copies ran while one was open for 5% of the time, Pallas kernels for 0%

commit v1 on v0

--- a/solution.py
+++ b/solution.py
@@ -119,7 +119,15 @@
         jnp.zeros((kv_heads, query_rows), jnp.float32),
         jnp.zeros((kv_heads, query_rows, head_dim), jnp.float32),
     )
-    kv_piece = lax.all_gather(stacked, "expert", axis=0, tiled=True)
+    kv_piece = jnp.concatenate(
+        lax.all_to_all(
+            jnp.stack(lax.psum(1, axis_name="expert") * [stacked]),
+            axis_name="expert",
+            split_axis=0,
+            concat_axis=0,
+        ),
+        axis=0,
+    )
     key_rows = kv_piece.shape[0]
     key_block = math.gcd(key_rows, 1024)
     blocks = kv_piece.reshape(key_rows // key_block, key_block, 2, kv_heads, head_dim)

time: 573 us -> 587 us (1.024)
  waiting for transfers between devices: 233 us -> 255 us
  local copies, waits for them, and re-layouts: 110 us -> 124 us
  between operations: 16.1 us -> 2.32 us
    all_to_all x0 -> x1, waiting for transfers between devices: none -> 102 us  [body(): lax.all_to_all(jnp.stack(lax.psum(1, axis_name='expert') * [stacked]), ax...]
    all_gather x1 -> x0, waiting for transfers between devices: 90.7 us -> none  [body(): kv_piece = lax.all_gather(stacked, 'expert', axis=0, tiled=True)]
    another operation x2 -> x4, local copies, waits for them, and re-layouts: 0.09 us -> 18.7 us  [the longest x1 13.3 us: body(): kv_piece.reshape(key_rows // key_block, key_block, 2, kv_heads, head_dim)]
    unnamed x24 -> x23, local copies, waits for them, and re-layouts: 32.8 us -> 16.3 us
    all_to_all x0 -> x1, local copies, waits for them, and re-layouts: none -> 12 us  [body(): lax.all_to_all(jnp.stack(lax.psum(1, axis_name='expert') * [stacked]), ax...]
    all_gather x1 -> x0, starting transfers between devices: 10.4 us -> none  [body(): kv_piece = lax.all_gather(stacked, 'expert', axis=0, tiled=True)]
    all_to_all x1, waiting for transfers between devices: 66.1 us -> 76.4 us  [body(): lax.all_to_all(combined.astype(jnp.bfloat16), 'expert', split_axis=0, con...]
    all_to_all x0 -> x1, starting transfers between devices: none -> 8.07 us  [body(): lax.all_to_all(jnp.stack(lax.psum(1, axis_name='expert') * [stacked]), ax...]
where the time goes in v1:
time: 587 us; the launch traced here: 582 us
  waiting for transfers between devices  255 us (43%)
  local copies, waits for them, and re-layouts  124 us (21%)
  other arithmetic  84.6 us (14%)
  matrix products  60.3 us (10%)
  starting transfers between devices  27.8 us (5%)
  Pallas kernels  27.5 us (5%)
    all_to_all x1, waiting for transfers between devices, body(): lax.all_to_all(jnp.stack(lax.psum(1, axis_name='expert') * [stacked]), ax...  102 us
    all_to_all x1, waiting for transfers between devices, body(): lax.all_to_all(combined.astype(jnp.bfloat16), 'expert', split_axis=0, con...  76.4 us
    all_to_all x1, waiting for transfers between devices, body(): lax.all_to_all(outgoing, 'expert', split_axis=0, concat_axis=0, tiled=True)  57 us
    reduce_sum x8, other arithmetic, step_block(): totals_out = totals_in * rescale + jnp.sum(weights, axis=-1)  39.3 us
    dot_general x8, matrix products, step_block(): jnp.einsum('hrd,khd->hrk', grouped_queries, kv_block[:, 0], preferred_ele...  35.7 us
    another operation x2, Pallas kernels  26.2 us
    ppermute x1, waiting for transfers between devices, from_partner(): return lax.ppermute(block, axis, route)  19.4 us
    dot_general x8, matrix products, step_block(): jnp.einsum('hrk,khd->hrd', weights.astype(jnp.bfloat16), kv_block[:, 1],...  19.1 us
  transfers between devices with their start and end apart: 4, of which 4 were waited for; matrix products, arithmetic and copies ran while one was open for 5% of the time, Pallas kernels for 0%

profile of v1, /device:TPU:0, one launch (start us, length us, event | category | flops | bytes accessed | tf_op | source)
XLA Modules:
  0.0 582.3 jit_solution(15908903539385611907)
XLA Ops:
  2.3 18.0 %reduce-window.6 = s32[64,8,128]{2,1,0:T(8,128)S(1)} reduce-window(s32[64,8,128]{2,1,0:T(8,128)S(1)} %fusion.22, s32[]{:T(128)} %constant.32.clone.1), window={size=1x1x128 pad=0_0x0_0x127_0}, to_apply=%region_0.0 | reduce-window | flops 8323072 | bytes 524292 | tf_op jit(solution)/shard_map/reduce-window
  21.2 4.3 scatter_custom_fusion
  25.5 1.1 concatenate.4
  26.6 7.1 %gather_fusion = bf16[1536,2048]{1,0:T(8,128)(2,1)} fusion(bf16[129,2048]{1,0:T(8,128)(2,1)S(1)} %concatenate.4, s32[2048]{0:T(1024)S(1)} %pad_clamp_fusion), kind=kCustom, calls=%fused_computation | custom fusion | bytes 12589056 | tf_op jit(solution)/shard_map/gather | solution.py:73
  33.7 11.9 %all-to-all-start = ((bf16[64,24,2048]{2,1,0:T(8,128)(2,1)}), bf16[64,24,2048]{2,1,0:T(8,128)(2,1)}, u32[]{:S(2)}, u32[]{:S(2)}) async-start(bf16[64,24,2048]{2,1,0:T(8,128)(2,1)} %bitcast.106), calls=%async_computation | async-start | bytes 12582912 | tf_op jit(solution)/shard_map/all_to_all | solution.py:75
  45.7 2.0 sort.31
  50.3 1.3 ragged-dot-metadata
  51.6 14.6 %reshape.137 = bf16[2,2048,768]{2,1,0:T(8,128)(2,1)} reshape(bf16[2,2048,2,384]{3,2,1,0:T(2,128)(2,1)} %param.17) | data formatting | bytes 12582912 | tf_op jit(solution)/shard_map/reshape | solution.py:36
  66.2 2.0 sort.32
  68.3 57.0 %all-to-all-done = bf16[64,24,2048]{2,1,0:T(8,128)(2,1)} async-done(((bf16[64,24,2048]{2,1,0:T(8,128)(2,1)}), bf16[64,24,2048]{2,1,0:T(8,128)(2,1)}, u32[]{:S(2)}, u32[]{:S(2)}) %all-to-all-start) | async-done | bytes 6291488 | tf_op jit(solution)/shard_map/all_to_all | solution.py:75
  125.3 6.4 %gather_fusion.1 = bf16[64,24,2048]{2,1,0:T(8,128)(2,1)} fusion(bf16[64,24,2048]{2,1,0:T(8,128)(2,1)} %all-to-all-done, s32[1024]{0:T(1024)S(1)} %pad_clamp_fusion.2), kind=kCustom, calls=%fused_computation.1 | custom fusion | bytes 12583168 | tf_op jit(solution)/shard_map/gather | solution.py:31
  131.7 13.9 %ragged-dot-none.1 = f32[1536,768]{1,0:T(8,128)} custom-call(s32[1]{0:T(128)} %get-tuple-element.41, s32[3]{0:T(128)} %get-tuple-element.42, s32[7]{0:T(128)} %get-tuple-element.43, s32[7]{0:T(128)} %get-tuple-element.44, s32[1]{0:T(128)} %get-tuple-element.41, bf16[1536,2048]{1,0:T(8,128)(2,1)} %bitcast.111, bf16[2,2048,768]{2,1,0:T(8,128)(2,1)} %reshape.137), custom_call_target="tpu_custom_call" | custom-call | flops 4831838208 | bytes 17301512 | tf_op jit(solution)/shard_map/ragged_dot_general/ragged-dot-none
  145.6 4.1 fusion.15
  149.7 12.3 %ragged-dot-none = f32[1536,2048]{1,0:T(8,128)} custom-call(s32[1]{0:T(128)} %get-tuple-element.41, s32[3]{0:T(128)} %get-tuple-element.42, s32[7]{0:T(128)} %get-tuple-element.43, s32[7]{0:T(128)} %get-tuple-element.44, s32[1]{0:T(128)} %get-tuple-element.41, bf16[1536,384]{1,0:T(8,128)(2,1)} %fusion.15, bf16[2,384,2048]{2,1,0:T(8,128)(2,1)} %param.18), custom_call_target="tpu_custom_call" | custom-call | flops 2415919104 | bytes 16908296 | tf_op jit(solution)/shard_map/ragged_dot_general/ragged-dot-none
  162.0 10.4 %gather_fusion.2 = f32[64,24,2048]{2,1,0:T(8,128)} fusion(f32[64,24,2048]{2,1,0:T(8,128)} %bitcast.105, s32[1024]{0:T(1024)S(1)} %pad_clamp_fusion.1), kind=kCustom, calls=%fused_computation.2 | custom fusion | bytes 25166080 | tf_op jit(solution)/shard_map/gather | solution.py:44
  172.4 19.4 %collective-permute-done = f32[64,24,2048]{2,1,0:T(8,128)S(1)} collective-permute-done((f32[64,24,2048]{2,1,0:T(8,128)}, f32[64,24,2048]{2,1,0:T(8,128)S(1)}, u32[]{:S(2)}, u32[]{:S(2)}) %collective-permute-start) | collective-permute-done | bytes 12582944 | tf_op jit(solution)/shard_map/ppermute | solution.py:17
  191.8 8.5 %add_convert_fusion = bf16[64,24,2048]{2,1,0:T(8,128)(2,1)} fusion(f32[64,24,2048]{2,1,0:T(8,128)} %gather_fusion.2, f32[64,24,2048]{2,1,0:T(8,128)S(1)} %collective-permute-done), kind=kLoop, calls=%fused_computation.25 | loop fusion | flops 6291456 | bytes 31457280 | tf_op jit(solution)/shard_map/convert_element_type | solution.py:82
  200.3 7.8 %all-to-all-start.1 = ((bf16[64,24,2048]{2,1,0:T(8,128)(2,1)}), bf16[64,24,2048]{2,1,0:T(8,128)(2,1)}, u32[]{:S(2)}, u32[]{:S(2)}) async-start(bf16[64,24,2048]{2,1,0:T(8,128)(2,1)} %add_convert_fusion), calls=%async_computation.1 | async-start | bytes 12582912 | tf_op jit(solution)/shard_map/all_to_all | solution.py:81
  208.2 2.0 copy.74
  210.3 2.5 copy.64
  212.8 76.4 %all-to-all-done.1 = bf16[64,24,2048]{2,1,0:T(8,128)(2,1)} async-done(((bf16[64,24,2048]{2,1,0:T(8,128)(2,1)}), bf16[64,24,2048]{2,1,0:T(8,128)(2,1)}, u32[]{:S(2)}, u32[]{:S(2)}) %all-to-all-start.1) | async-done | bytes 6291488 | tf_op jit(solution)/shard_map/all_to_all | solution.py:81
  289.2 12.5 %gather_fusion.3 = bf16[1024,2048]{1,0:T(8,128)(2,1)} fusion(bf16[1536,2048]{1,0:T(8,128)(2,1)} %bitcast.10, s32[1024]{0:T(1024)S(1)} %broadcast_clamp_fusion), kind=kCustom, calls=%fused_computation.3 | custom fusion | bytes 8392704 | tf_op jit(solution)/shard_map/gather | solution.py:86
  301.6 6.6 %fusion.14 = f32[128,2048]{1,0:T(8,128)S(1)} fusion(bf16[1024,2048]{1,0:T(8,128)(2,1)} %gather_fusion.3, f32[128,8]{1,0:T(8,128)S(1)} %copy.63), kind=kLoop, calls=%fused_computation.27 | loop fusion | flops 6029312 | bytes 5246976 | tf_op jit(solution)/shard_map/reduce_sum | solution.py:90
  309.5 5.3 stack.27
  314.8 8.1 %all-to-all-start.2 = ((bf16[64,128,2,256]{1,3,2,0:T(8,128)(2,1)}), bf16[64,128,2,256]{1,3,2,0:T(8,128)(2,1)}, u32[]{:S(2)}, u32[]{:S(2)}) async-start(bf16[64,128,2,256]{1,3,2,0:T(8,128)(2,1)} %stack.27), calls=%async_computation.2 | async-start | bytes 16777216 | tf_op jit(solution)/shard_map/all_to_all | solution.py:123
  322.9 4.7 fusion.29
  329.2 102.4 %all-to-all-done.2 = bf16[64,128,2,256]{1,3,2,0:T(8,128)(2,1)} async-done(((bf16[64,128,2,256]{1,3,2,0:T(8,128)(2,1)}), bf16[64,128,2,256]{1,3,2,0:T(8,128)(2,1)}, u32[]{:S(2)}, u32[]{:S(2)}) %all-to-all-start.2) | async-done | bytes 8388640 | tf_op jit(solution)/shard_map/all_to_all | solution.py:123
  431.6 12.0 %copy.65 = bf16[64,128,2,256]{1,0,3,2:T(8,128)(2,1)} copy(bf16[64,128,2,256]{1,3,2,0:T(8,128)(2,1)} %all-to-all-done.2) | data formatting | bytes 16777216 | tf_op jit(solution)/shard_map/all_to_all | solution.py:123
  443.6 13.3 %reshape_reshape.3 = bf16[8,1024,2,2,128]{1,0,4,3,2:T(8,128)(2,1)} reshape(bf16[64,128,2,256]{1,0,3,2:T(8,128)(2,1)} %copy.65) | data formatting | bytes 16777216 | tf_op jit(solution)/shard_map/reshape;reshape | solution.py:133
  456.9 12.0 %copy.69 = bf16[8,1024,2,2,128]{4,1,3,2,0:T(8,128)(2,1)} copy(bf16[8,1024,2,2,128]{1,0,4,3,2:T(8,128)(2,1)} %reshape_reshape.3) | data formatting | bytes 16777216
  468.9 111.7 %while.15 = (s32[]{:T(128)}, f32[2,1024]{1,0:T(2,128)S(1)}, f32[2,1024]{1,0:T(2,128)S(1)}, f32[2,1024,128]{2,1,0:T(8,128)S(1)}, bf16[8,1024,2,2,128]{4,1,3,2,0:T...) while((s32[]{:T(128)}, f32[2,1024]{1,0:T(2,128)S(1)}, ...), condition=%wide.region_14.15_spmd.clone, body=%wide.region_11.14_spmd.clone.sunk | while | flops 1091315712 | bytes 64618624 | solution.py:155
  468.9 1.3 dynamic-slice_bitcast_fusion.2
  470.2 4.5 bitcast_reduce_fusion.2
  474.7 4.9 fusion.42
  480.4 2.4 fusion.44
  482.9 1.3 dynamic-slice_bitcast_fusion.2
  484.2 4.5 bitcast_reduce_fusion.2
  488.7 4.9 fusion.42
  494.4 2.4 fusion.44
  496.8 1.3 dynamic-slice_bitcast_fusion.2
  498.1 4.5 bitcast_reduce_fusion.2
  502.6 4.9 fusion.42
  508.4 2.4 fusion.44
  510.8 1.3 dynamic-slice_bitcast_fusion.2
  512.1 4.5 bitcast_reduce_fusion.2
  516.6 4.9 fusion.42
  522.3 2.4 fusion.44
  524.8 1.3 dynamic-slice_bitcast_fusion.2
  526.1 4.5 bitcast_reduce_fusion.2
  530.6 4.9 fusion.42
  536.3 2.4 fusion.44
  538.7 1.3 dynamic-slice_bitcast_fusion.2
  540.0 4.5 bitcast_reduce_fusion.2
  544.5 4.9 fusion.42
  550.3 2.4 fusion.44
  552.7 1.3 dynamic-slice_bitcast_fusion.2
  554.0 4.5 bitcast_reduce_fusion.2
  558.5 4.9 fusion.42
  564.3 2.4 fusion.44
  566.7 1.3 dynamic-slice_bitcast_fusion.2
  568.0 4.5 bitcast_reduce_fusion.2
  572.5 4.9 fusion.42
  578.2 2.4 fusion.44
  581.3 0.9 copy.80
  (108 shorter events, 14.2 us)
Async XLA Ops:
  33.7 11.9 %copy-start.5 = (s32[8192]{0:T(1024)S(1)}, s32[8192]{0:T(1024)}, u32[]{:S(2)}) copy-start(s32[8192]{0:T(1024)} %param.14) | copy-start | bytes 98308
  33.7 91.6 %all-to-all-start = ((bf16[64,24,2048]{2,1,0:T(8,128)(2,1)}), bf16[64,24,2048]{2,1,0:T(8,128)(2,1)}, u32[]{:S(2)}, u32[]{:S(2)}) async-start(bf16[64,24,2048]{2,1,0:T(8,128)(2,1)} %bitcast.106), calls=%async_computation | async-start | bytes 12582912 | tf_op jit(solution)/shard_map/all_to_all | solution.py:75
  172.4 19.4 %collective-permute-start = (f32[64,24,2048]{2,1,0:T(8,128)}, f32[64,24,2048]{2,1,0:T(8,128)S(1)}, u32[]{:S(2)}, u32[]{:S(2)}) collective-permute-start(f32[64,24,2048]{2,1,0:T(8,128)} %gather_fusion.2), channel_id=1, source_target_pairs={{0,1},{1,0},{2,3},{3,2},{4,5},{5,4},{6,7},{7,6},{8,9},{9,8},{10,11... | collective-permute-start | bytes 37748744 | tf_op jit(solution)/shard_map/ppermute | solution.py:17
  200.3 7.9 %copy-start.6 = (f32[128,8]{0,1:T(8,128)S(1)}, f32[128,8]{0,1:T(8,128)}, u32[]{:S(2)}) copy-start(f32[128,8]{0,1:T(8,128)} %param.16) | copy-start | bytes 12292
  200.3 88.9 %all-to-all-start.1 = ((bf16[64,24,2048]{2,1,0:T(8,128)(2,1)}), bf16[64,24,2048]{2,1,0:T(8,128)(2,1)}, u32[]{:S(2)}, u32[]{:S(2)}) async-start(bf16[64,24,2048]{2,1,0:T(8,128)(2,1)} %add_convert_fusion), calls=%async_computation.1 | async-start | bytes 12582912 | tf_op jit(solution)/shard_map/all_to_all | solution.py:81
  289.2 19.1 %copy-start.3 = (bf16[128,2048]{1,0:T(8,128)(2,1)S(1)}, bf16[128,2048]{1,0:T(8,128)(2,1)}, u32[]{:S(2)}) copy-start(bf16[128,2048]{1,0:T(8,128)(2,1)} %param.13) | copy-start | bytes 1572868
  301.6 6.9 %copy-start.2 = (bf16[512,2048]{1,0:T(8,128)(2,1)S(1)}, bf16[512,2048]{1,0:T(8,128)(2,1)}, u32[]{:S(2)}) copy-start(bf16[512,2048]{1,0:T(8,128)(2,1)} %copy.64) | copy-start | bytes 6291460
  301.6 6.9 %copy-start.4 = (f32[2048]{0:T(1024)S(1)}, f32[2048]{0:T(1024)}, u32[]{:S(2)}) copy-start(f32[2048]{0:T(1024)} %param.19) | copy-start | bytes 24580
  301.6 7.8 %copy-start.8 = (f32[128]{0:T(128)S(1)}, f32[128]{0:T(128)}, u32[]{:S(2)}) copy-start(f32[128]{0:T(128)} %param.23) | copy-start | bytes 1540
  308.5 14.4 %copy-start.1 = (f32[128,2048]{1,0:T(8,128)}, f32[128,2048]{1,0:T(8,128)S(1)}, u32[]{:S(2)}) copy-start(f32[128,2048]{1,0:T(8,128)S(1)} %get-tuple-element.109) | copy-start | bytes 3145732
  314.8 116.8 %all-to-all-start.2 = ((bf16[64,128,2,256]{1,3,2,0:T(8,128)(2,1)}), bf16[64,128,2,256]{1,3,2,0:T(8,128)(2,1)}, u32[]{:S(2)}, u32[]{:S(2)}) async-start(bf16[64,128,2,256]{1,3,2,0:T(8,128)(2,1)} %stack.27), calls=%async_computation.2 | async-start | bytes 16777216 | tf_op jit(solution)/shard_map/all_to_all | solution.py:123
  327.6 1.1 copy-start.7
  474.7 5.8 copy-start
  488.6 5.8 copy-start
  502.6 5.8 copy-start
  516.6 5.8 copy-start
  530.5 5.8 copy-start
  544.5 5.8 copy-start
  558.5 5.8 copy-start
  572.4 5.8 copy-start
